TPU v7x, 512 devices: a whole 4x4x16 slice. The times are simulated.
512 devices in a mesh: ctx: 32 (over z, core), chan: 4 (over x), dp: 4 (over y).
Axes of the slice: x: 4, y: 4, z: 16, core: 2. Of those that a mesh axis runs over, the one named last changes fastest.
Arguments:
- projected: bfloat16 [3, 16384, 8192], P(None, ('dp', 'ctx'), 'chan'), parts along dimension 1, may hold values from -6 to 6
- short_weight: float32 [7, 3, 8192], P(None, None, 'chan'), may hold values from -2 to 2
- pos_in: float32 [33, 64], replicated, may hold values from -1 to 1
- pos_bias: float32 [64], replicated, may hold values from -4 to 4
- sine_freq: float32 [64], replicated, may hold values from 1.5 to 3
- pos_mid: float32 [64, 64], replicated, may hold values from -0.75 to 0.75
- pos_out: float32 [64, 8192], P(None, 'chan'), may hold values from -0.75 to 0.75
- decay_rate: float32 [8192], P('chan'), may hold values from 2.4414063e-05 to 0.05
- skip_gain: float32 [8192], P('chan'), may hold values from -4 to 4
Outputs:
- mixed: bfloat16 [16384, 8192], P(('dp', 'ctx'), 'chan'), parts along dimension 0
There are 4 independent parts, one for each index of `dp`. A program takes and returns all parts, laid end to end along the dimension named above; an argument that names none is the same for every part. Nothing has to cross between parts.
All inputs are finite; a program needn't handle non-finite values.
Results may differ from a plain program's by a relative error of at most 0.001.
Values may be sent and summed in bfloat16 or wider, within the bound.
A program may use at most 128 MiB of HBM per device.

v0:
```python
import math

import jax
import jax.numpy as jnp
from jax import lax
from jax.sharding import PartitionSpec as P

BANDS = 16
TAPS = 7


HIGHEST = lax.Precision.HIGHEST


def shifted(x, axis, by):
    size = lax.axis_size(axis)
    pairs = [(i, i + by) for i in range(size) if 0 <= i + by < size]
    return lax.ppermute(x, axis, pairs)


def features(positions, total_len):
    band_ids = jnp.arange(1, BANDS + 1, dtype=jnp.float32)
    angles = positions[:, None] * band_ids[None, :] * (2.0 * math.pi / total_len)
    return jnp.concatenate(
        [positions[:, None] / total_len, jnp.cos(angles), jnp.sin(angles)], axis=1
    )


def filter_rows(positions, total_len, pos_in, pos_bias, sine_freq, pos_mid, pos_out, decay_rate):
    inputs = features(positions, total_len)
    first_layer = jnp.sin(
        sine_freq
        * (
            jnp.dot(inputs, pos_in, precision=HIGHEST, preferred_element_type=jnp.float32)
            + pos_bias
        )
    )
    second_layer = jnp.sin(
        sine_freq
        * jnp.dot(first_layer, pos_mid, precision=HIGHEST, preferred_element_type=jnp.float32)
    )
    raw_filter = jnp.dot(
        second_layer, pos_out, precision=HIGHEST, preferred_element_type=jnp.float32
    )
    return raw_filter * jnp.exp(-decay_rate[None, :] * positions[:, None])


def turn_table(outer_ids, inner_ids, modulus):
    product_grid = outer_ids[:, None] * inner_ids[None, :] % modulus
    angles = product_grid.astype(jnp.float32) * (2.0 * math.pi / modulus)
    return (jnp.cos(angles), jnp.sin(angles))


def section_outer(table, data):
    return jnp.einsum(
        "ka,cab->ckb", table, data, precision=HIGHEST, preferred_element_type=jnp.float32
    )


def section_inner(table, data):
    return jnp.einsum(
        "ckb,bj->ckj", data, table, precision=HIGHEST, preferred_element_type=jnp.float32
    )


def padded_spectrum(signal, outer_count, inner_count, tables):
    cos_half, sin_half, cos_twist, sin_twist, cos_inner, sin_inner = tables
    shaped = signal.reshape(signal.shape[0], outer_count // 2, inner_count)
    real_one = section_outer(cos_half, shaped)
    imag_one = -section_outer(sin_half, shaped)
    real_two = real_one * cos_twist + imag_one * sin_twist
    imag_two = imag_one * cos_twist - real_one * sin_twist
    spec_real = section_inner(cos_inner, real_two) + section_inner(sin_inner, imag_two)
    spec_imag = section_inner(cos_inner, imag_two) - section_inner(sin_inner, real_two)
    return (spec_real, spec_imag)


def causal_local(driven_cols, normed_cols, total_len):
    full_len = 2 * total_len
    inner_count = math.gcd(total_len, 128)
    outer_count = full_len // inner_count
    outer_full = jnp.arange(outer_count, dtype=jnp.int32)
    outer_half = jnp.arange(outer_count // 2, dtype=jnp.int32)
    inner_ids = jnp.arange(inner_count, dtype=jnp.int32)
    cos_half, sin_half = turn_table(outer_full, outer_half, outer_count)
    cos_twist, sin_twist = turn_table(outer_full, inner_ids, full_len)
    cos_inner, sin_inner = turn_table(inner_ids, inner_ids, inner_count)
    tables = (cos_half, sin_half, cos_twist, sin_twist, cos_inner, sin_inner)
    sig_real, sig_imag = padded_spectrum(driven_cols, outer_count, inner_count, tables)
    fil_real, fil_imag = padded_spectrum(normed_cols, outer_count, inner_count, tables)
    prod_real = sig_real * fil_real - sig_imag * fil_imag
    prod_imag = sig_real * fil_imag + sig_imag * fil_real
    back_real = section_inner(cos_inner, prod_real) - section_inner(sin_inner, prod_imag)
    back_imag = section_inner(sin_inner, prod_real) + section_inner(cos_inner, prod_imag)
    turned_real = back_real * cos_twist - back_imag * sin_twist
    turned_imag = back_real * sin_twist + back_imag * cos_twist
    cos_last, sin_last = turn_table(outer_half, outer_full, outer_count)
    result = (
        section_outer(cos_last, turned_real) - section_outer(sin_last, turned_imag)
    ) / full_len
    return result.reshape(driven_cols.shape[0], total_len)


def body(
    projected, short_weight, pos_in, pos_bias, sine_freq, pos_mid, pos_out, decay_rate, skip_gain
):
    ctx_count = lax.axis_size("ctx")
    ctx_place = lax.axis_index("ctx")
    block_rows = projected.shape[1]
    total_len = block_rows * ctx_count
    rim_rows = shifted(projected[:, block_rows - (TAPS - 1) :, :], "ctx", 1)
    extended = jnp.concatenate([rim_rows, projected], axis=1)
    short_out = jnp.zeros(projected.shape, jnp.float32)
    for tap_index in range(TAPS):
        offset = TAPS - 1 - tap_index
        short_out = short_out + short_weight[tap_index][:, None, :] * extended[
            :, offset : offset + block_rows, :
        ].astype(jnp.float32)
    left_gate, right_gate, value_stream = (short_out[0], short_out[1], short_out[2])
    driven = left_gate * value_stream
    own_width = driven.shape[1] // ctx_count
    driven_cols = lax.all_to_all(driven.T, "ctx", split_axis=0, concat_axis=1, tiled=True)
    own_out = lax.dynamic_slice_in_dim(pos_out, ctx_place * own_width, own_width, 1)
    own_decay = lax.dynamic_slice_in_dim(decay_rate, ctx_place * own_width, own_width, 0)
    positions = jnp.arange(total_len, dtype=jnp.int32).astype(jnp.float32)
    long_filter = filter_rows(
        positions, total_len, pos_in, pos_bias, sine_freq, pos_mid, own_out, own_decay
    )
    normed = long_filter / jnp.sqrt(jnp.sum(long_filter * long_filter, axis=0) + 1e-05)
    conv_cols = causal_local(driven_cols, normed.T, total_len)
    long_conv = lax.all_to_all(conv_cols, "ctx", split_axis=1, concat_axis=0, tiled=True).T
    return (right_gate * (long_conv + skip_gain[None, :] * driven)).astype(jnp.bfloat16)


def solution(mesh):
    placed = (
        P(None, ("dp", "ctx"), "chan"),
        P(None, None, "chan"),
        P(),
        P(),
        P(),
        P(),
        P(None, "chan"),
        P("chan"),
        P("chan"),
    )
    return jax.shard_map(
        body, mesh=mesh, in_specs=placed, out_specs=P(("dp", "ctx"), "chan"), check_vma=False
    )
```

profile of v0, /device:TPU:1, one launch (start us, length us, event | category | flops | bytes accessed | tf_op | source)
XLA Modules:
  0.0 186.8 jit_solution(15582704545788772176)
XLA Ops:
  0.0 0.0 copy-start
  0.0 0.0 copy-start.5
  0.0 1.0 slice.53
  1.0 4.9 %collective-permute-start = (bf16[3,6,2048]{2,1,0:T(8,128)(2,1)S(1)}, bf16[3,6,2048]{2,1,0:T(8,128)(2,1)S(1)}, u32[]{:S(2)}, u32[]{:S(2)}) collective-permute-start(bf16[3,6,2048]{2,1,0:T(8,128)(2,1)S(1)} %slice.53), channel_id=1, source_target_pairs={{0,16},{16,32},{32,48},{48,64},{64,80},{80,96},{96,112},{112,128},... | collective-permute-start | bytes 221192 | tf_op jit(solution)/shard_map/ppermute | solution.py:18
  6.0 1.9 %copy.16 = bf16[3,128,2048]{1,2,0:T(8,128)(2,1)S(1)} copy(bf16[3,128,2048]{2,1,0:T(8,128)(2,1)} %param.9) | data formatting | bytes 3145728 | tf_op args[0]
  7.9 0.0 copy-done.5
  7.9 0.1 fusion.210
  8.2 1.0 fusion.61
  9.2 0.8 dynamic-slice_negate_fusion
  9.9 0.0 collective-permute-done
  9.9 1.6 copy.17
  11.5 13.3 %multiply_add_fusion = f32[3,128,2048]{1,2,0:T(8,128)S(1)} fusion(bf16[3,128,2048]{1,2,0:T(8,128)(2,1)S(1)} %copy.16, bf16[3,6,2048]{1,2,0:T(8,128)(2,1)} %copy.17, f32[3,2048]{1,0:T(4,128)S(1)} %get-tuple-element.18, f32[3,2048]{1,0:T(4,128)S(1)} %get-tuple-element.19, f32[3,2048]{1,0:T(4,128)S(1)} %get-tuple-element.20, ...), kind=kLoop, calls=%fused_computation.15 | loop fusion | flops 29884416 | bytes 4964352 | tf_op jit(solution)/shard_map/add | solution.py:116
  24.9 0.0 copy-start.1
  24.9 1.6 copy-done.1
  26.5 0.0 copy-start.7
  26.5 0.0 copy-start.9
  26.5 0.0 copy-start.10
  26.5 1.2 slice_multiply_fusion
  27.7 0.0 copy-start.6
  27.7 15.5 %all-to-all-start = ((f32[32,64,128]{2,1,0:T(8,128)}), f32[32,64,128]{2,1,0:T(8,128)S(1)}, u32[]{:S(2)}, u32[]{:S(2)}) async-start(f32[32,64,128]{2,1,0:T(8,128)} %bitcast.3), calls=%async_computation | async-start | bytes 2097152 | tf_op jit(solution)/shard_map/all_to_all | solution.py:122
  43.3 0.0 copy-done.7
  43.3 0.0 copy-done.9
  43.3 0.0 copy-done.10
  43.3 4.4 %fusion.1 = f32[4096,64]{0,1:T(8,128)S(1)} fusion(f32[33,64]{1,0:T(8,128)S(1)} %copy-done.7, f32[4096,16]{0,1:T(8,128)S(1)} %get-tuple-element.15, f32[4096,16]{0,1:T(8,128)S(1)} %get-tuple-element.14, f32[4096,1]{0,1:T(1,128)S(1)} %convert_multiply_fusion, f32[64]{0:T(128)S(1)} %copy-done.10, f32[64]{0:T(128)S(1)} %copy-done.9), kind=kOutput, calls=%fused_computation.13 | convolution fusion | flops 104603648 | bytes 1598208 | tf_op jit(solution)/shard_map/dot_general | solution.py:34
  47.7 0.0 copy-done.6
  47.7 4.4 %fusion.2 = f32[4096,64]{0,1:T(8,128)S(1)} fusion(f32[4096,64]{0,1:T(8,128)S(1)} %fusion.1, f32[64,64]{1,0:T(8,128)S(1)} %copy-done.6, f32[64]{0:T(128)S(1)} %copy-done.9), kind=kOutput, calls=%fused_computation.14 | convolution fusion | flops 201588736 | bytes 2113792 | tf_op jit(solution)/shard_map/dot_general | solution.py:40
  52.1 0.0 copy-done
  52.1 1.3 multiply_reduce_fusion
  53.4 0.3 fusion.32
  53.7 0.2 copy.29
  53.9 0.1 fusion.122
  54.0 2.1 %fusion.112 = f32[64,128,64]{1,2,0:T(8,128)S(1)} fusion(f32[64,32,128]{2,1,0:T(8,128)S(1)} %bitcast.155), kind=kOutput, calls=%fused_computation.142 | convolution fusion | flops 201355264 | bytes 3145728 | tf_op jit(solution)/shard_map/ka,cab->ckb/dot_general | solution.py:55
  56.1 1.9 %fusion.115 = f32[64,128,64]{1,2,0:T(8,128)S(1)} fusion(f32[64,32,128]{2,1,0:T(8,128)S(1)} %bitcast.156), kind=kOutput, calls=%fused_computation.145 | convolution fusion | flops 201355264 | bytes 3145728 | tf_op jit(solution)/shard_map/ka,cab->ckb/dot_general | solution.py:55
  58.0 2.2 %fusion.54 = f32[64,64,128]{2,1,0:T(8,128)S(1)} fusion(f32[64,128,64]{1,2,0:T(8,128)S(1)} %fusion.115, f32[64,128,64]{1,2,0:T(8,128)S(1)} %fusion.112, f32[64,128]{1,0:T(8,128)S(1)} %get-tuple-element.24, f32[64,128]{1,0:T(8,128)S(1)} %get-tuple-element.25), kind=kOutput, calls=%fused_computation.80 | convolution fusion | flops 807632896 | bytes 6356992 | tf_op jit(solution)/shard_map/ckb,bj->ckj/dot_general | solution.py:61
  60.3 2.2 %fusion.58 = f32[64,64,128]{2,1,0:T(8,128)S(1)} fusion(f32[64,128,64]{1,2,0:T(8,128)S(1)} %fusion.115, f32[64,128,64]{1,2,0:T(8,128)S(1)} %fusion.112, f32[64,128]{1,0:T(8,128)S(1)} %get-tuple-element.24, f32[64,128]{1,0:T(8,128)S(1)} %get-tuple-element.25), kind=kOutput, calls=%fused_computation.81 | convolution fusion | flops 807632896 | bytes 6356992 | tf_op jit(solution)/shard_map/ckb,bj->ckj/dot_general | solution.py:61
  62.5 3.6 %convolution_subtract_fusion.1 = f32[64,64,128]{2,1,0:T(8,128)} fusion(f32[64,64,128]{2,1,0:T(8,128)S(1)} %fusion.54, f32[64,128,64]{1,2,0:T(8,128)S(1)} %fusion.115, f32[64,128,64]{1,2,0:T(8,128)S(1)} %fusion.112, f32[64,128]{1,0:T(8,128)S(1)} %get-tuple-element.24, f32[64,128]{1,0:T(8,128)S(1)} %get-tuple-element.25), kind=kOutput, calls=%fused_computation.40 | convolution fusion | flops 808157184 | bytes 8454144 | tf_op jit(solution)/shard_map/ckb,bj->ckj/dot_general | solution.py:61
  66.1 3.6 %convolution_add_fusion.2 = f32[64,64,128]{2,1,0:T(8,128)} fusion(f32[64,64,128]{2,1,0:T(8,128)S(1)} %fusion.58, f32[64,128,64]{1,2,0:T(8,128)S(1)} %fusion.115, f32[64,128,64]{1,2,0:T(8,128)S(1)} %fusion.112, f32[64,128]{1,0:T(8,128)S(1)} %get-tuple-element.24, f32[64,128]{1,0:T(8,128)S(1)} %get-tuple-element.25), kind=kOutput, calls=%fused_computation.42 | convolution fusion | flops 808157184 | bytes 8454144 | tf_op jit(solution)/shard_map/ckb,bj->ckj/dot_general | solution.py:61
  69.6 28.9 %all-to-all-done = f32[32,64,128]{2,1,0:T(8,128)S(1)} async-done(((f32[32,64,128]{2,1,0:T(8,128)}), f32[32,64,128]{2,1,0:T(8,128)S(1)}, u32[]{:S(2)}, u32[]{:S(2)}) %all-to-all-start) | async-done | bytes 1048608 | tf_op jit(solution)/shard_map/all_to_all | solution.py:122
  98.5 3.0 %fusion.33 = f32[64,128,64]{1,2,0:T(8,128)S(1)} fusion(f32[32,64,128]{2,1,0:T(8,128)S(1)} %all-to-all-done), kind=kOutput, calls=%fused_computation.61 | convolution fusion | flops 201355264 | bytes 3145728 | tf_op jit(solution)/shard_map/ka,cab->ckb/dot_general | solution.py:55
  101.5 2.5 %fusion.35 = f32[64,128,64]{1,2,0:T(8,128)S(1)} fusion(f32[32,64,128]{2,1,0:T(8,128)S(1)} %all-to-all-done), kind=kOutput, calls=%fused_computation.63 | convolution fusion | flops 201355264 | bytes 3145728 | tf_op jit(solution)/shard_map/ka,cab->ckb/dot_general | solution.py:55
  104.0 2.2 %fusion.48 = f32[64,64,128]{2,1,0:T(8,128)S(1)} fusion(f32[64,128,64]{1,2,0:T(8,128)S(1)} %fusion.35, f32[64,128,64]{1,2,0:T(8,128)S(1)} %fusion.33, f32[64,128]{1,0:T(8,128)S(1)} %get-tuple-element.24, f32[64,128]{1,0:T(8,128)S(1)} %get-tuple-element.25), kind=kOutput, calls=%fused_computation.78 | convolution fusion | flops 807632896 | bytes 6356992 | tf_op jit(solution)/shard_map/ckb,bj->ckj/dot_general | solution.py:61
  106.2 2.2 %fusion.52 = f32[64,64,128]{2,1,0:T(8,128)S(1)} fusion(f32[64,128,64]{1,2,0:T(8,128)S(1)} %fusion.35, f32[64,128,64]{1,2,0:T(8,128)S(1)} %fusion.33, f32[64,128]{1,0:T(8,128)S(1)} %get-tuple-element.24, f32[64,128]{1,0:T(8,128)S(1)} %get-tuple-element.25), kind=kOutput, calls=%fused_computation.79 | convolution fusion | flops 807632896 | bytes 6356992 | tf_op jit(solution)/shard_map/ckb,bj->ckj/dot_general | solution.py:61
  108.5 0.0 copy-start.3
  108.5 0.0 copy-start.4
  108.5 2.3 %convolution_add_fusion.3 = f32[64,64,128]{2,1,0:T(8,128)S(1)} fusion(f32[64,64,128]{2,1,0:T(8,128)S(1)} %fusion.52, f32[64,128,64]{1,2,0:T(8,128)S(1)} %fusion.35, f32[64,128,64]{1,2,0:T(8,128)S(1)} %fusion.33, f32[64,128]{1,0:T(8,128)S(1)} %get-tuple-element.24, f32[64,128]{1,0:T(8,128)S(1)} %get-tuple-element.25), kind=kOutput, calls=%fused_computation.43 | convolution fusion | flops 808157184 | bytes 8454144 | tf_op jit(solution)/shard_map/ckb,bj->ckj/dot_general | solution.py:61
  110.7 0.0 copy-done.3
  110.8 0.0 copy-done.4
  110.8 2.9 %multiply_add_fusion.1 = (f32[64,64,128]{2,1,0:T(8,128)S(1)}, f32[64,64,128]{2,1,0:T(8,128)S(1)}) fusion(f32[64,64,128]{2,1,0:T(8,128)S(1)} %copy-done.4, f32[64,64,128]{2,1,0:T(8,128)S(1)} %convolution_add_fusion.3, f32[64,64,128]{2,1,0:T(8,128)S(1)} %copy-done.3, f32[64,64,128]{2,1,0:T(8,128)S(1)} %fusion.48, f32[64,128,64]{1,2,0:T(8,128)S(1)} %fusion.35, ...), kind=kOutput, calls=%fused_computation.36 | convolution fusion | flops 811302912 | bytes 16842752 | tf_op jit(solution)/shard_map/ckb,bj->ckj/dot_general | solution.py:61
  113.7 2.1 %fusion.65 = f32[64,64,128]{2,1,0:T(8,128)S(1)} fusion(f32[64,64,128]{2,1,0:T(8,128)S(1)} %get-tuple-element.6), kind=kOutput, calls=%fused_computation.91 | convolution fusion | flops 805535744 | bytes 4194304 | tf_op jit(solution)/shard_map/ckb,bj->ckj/dot_general | solution.py:61
  115.8 2.1 %fusion.73 = f32[64,64,128]{2,1,0:T(8,128)S(1)} fusion(f32[64,64,128]{2,1,0:T(8,128)S(1)} %get-tuple-element.6), kind=kOutput, calls=%fused_computation.99 | convolution fusion | flops 805535744 | bytes 4194304 | tf_op jit(solution)/shard_map/ckb,bj->ckj/dot_general | solution.py:61
  118.0 2.1 %convolution_add_fusion.1 = f32[64,64,128]{2,1,0:T(8,128)S(1)} fusion(f32[64,64,128]{2,1,0:T(8,128)S(1)} %fusion.65, f32[64,64,128]{2,1,0:T(8,128)S(1)} %get-tuple-element.5), kind=kOutput, calls=%fused_computation.38 | convolution fusion | flops 806060032 | bytes 6291456 | tf_op jit(solution)/shard_map/ckb,bj->ckj/dot_general | solution.py:61
  120.1 2.1 %convolution_subtract_fusion = f32[64,64,128]{2,1,0:T(8,128)S(1)} fusion(f32[64,64,128]{2,1,0:T(8,128)S(1)} %fusion.73, f32[64,64,128]{2,1,0:T(8,128)S(1)} %get-tuple-element.5), kind=kOutput, calls=%fused_computation.39 | convolution fusion | flops 806060032 | bytes 6291456 | tf_op jit(solution)/shard_map/ckb,bj->ckj/dot_general | solution.py:61
  122.2 1.6 fusion.7
  123.8 1.7 fusion.26
  125.5 0.0 copy-start.2
  125.5 0.0 copy-start.8
  125.5 0.6 copy.20
  126.1 59.1 %all_to_all.32 = f32[64,32,128]{2,0,1:T(8,128)S(1)} all-to-all(f32[64,32,128]{2,0,1:T(8,128)S(1)} %copy.20), channel_id=1, replica_groups=mesh['ctx'=32,'chan'=4,'dp'=4] {'ctx'}, dimensions={1} | all-to-all | bytes 2097152 | tf_op jit(solution)/shard_map/all_to_all | solution.py:131
  185.2 0.0 copy-done.2
  185.2 0.0 copy-done.8
  185.3 0.3 fusion.30
  185.6 1.0 copy.21
  (8 shorter events, 0.1 us)
Async XLA Ops:
  0.0 52.1 %copy-start = (f32[64,2048]{1,0:T(8,128)S(1)}, f32[64,2048]{1,0:T(8,128)}, u32[]{:S(2)}) copy-start(f32[64,2048]{1,0:T(8,128)} %param.15) | copy-start | bytes 1572868
  0.0 7.9 %copy-start.5 = (f32[7,3,2048]{2,0,1:T(8,128)S(1)}, f32[7,3,2048]{2,0,1:T(8,128)}, u32[]{:S(2)}) copy-start(f32[7,3,2048]{2,0,1:T(8,128)} %param.10) | copy-start | bytes 516100
  1.0 8.9 %collective-permute-start = (bf16[3,6,2048]{2,1,0:T(8,128)(2,1)S(1)}, bf16[3,6,2048]{2,1,0:T(8,128)(2,1)S(1)}, u32[]{:S(2)}, u32[]{:S(2)}) collective-permute-start(bf16[3,6,2048]{2,1,0:T(8,128)(2,1)S(1)} %slice.53), channel_id=1, source_target_pairs={{0,16},{16,32},{32,48},{48,64},{64,80},{80,96},{96,112},{112,128},... | collective-permute-start | bytes 221192 | tf_op jit(solution)/shard_map/ppermute | solution.py:18
  24.9 1.6 copy-start.1
  26.5 16.7 %copy-start.7 = (f32[33,64]{1,0:T(8,128)S(1)}, f32[33,64]{1,0:T(8,128)}, u32[]{:S(2)}) copy-start(f32[33,64]{1,0:T(8,128)} %param.11) | copy-start | bytes 25348
  26.5 16.7 %copy-start.9 = (f32[64]{0:T(128)S(1)}, f32[64]{0:T(128)}, u32[]{:S(2)}) copy-start(f32[64]{0:T(128)} %param.13) | copy-start | bytes 772
  26.5 16.8 %copy-start.10 = (f32[64]{0:T(128)S(1)}, f32[64]{0:T(128)}, u32[]{:S(2)}) copy-start(f32[64]{0:T(128)} %param.12) | copy-start | bytes 772
  27.7 20.0 %copy-start.6 = (f32[64,64]{1,0:T(8,128)S(1)}, f32[64,64]{1,0:T(8,128)}, u32[]{:S(2)}) copy-start(f32[64,64]{1,0:T(8,128)} %param.14) | copy-start | bytes 49156
  27.7 70.8 %all-to-all-start = ((f32[32,64,128]{2,1,0:T(8,128)}), f32[32,64,128]{2,1,0:T(8,128)S(1)}, u32[]{:S(2)}, u32[]{:S(2)}) async-start(f32[32,64,128]{2,1,0:T(8,128)} %bitcast.3), calls=%async_computation | async-start | bytes 2097152 | tf_op jit(solution)/shard_map/all_to_all | solution.py:122
  108.5 2.3 %copy-start.3 = (f32[64,64,128]{2,1,0:T(8,128)S(1)}, f32[64,64,128]{2,1,0:T(8,128)}, u32[]{:S(2)}) copy-start(f32[64,64,128]{2,1,0:T(8,128)} %convolution_subtract_fusion.1) | copy-start | bytes 6291460
  108.5 2.3 %copy-start.4 = (f32[64,64,128]{2,1,0:T(8,128)S(1)}, f32[64,64,128]{2,1,0:T(8,128)}, u32[]{:S(2)}) copy-start(f32[64,64,128]{2,1,0:T(8,128)} %convolution_add_fusion.2) | copy-start | bytes 6291460
  125.5 59.8 %copy-start.2 = (f32[3,128,2048]{1,2,0:T(8,128)S(1)}, f32[3,128,2048]{1,2,0:T(8,128)}, u32[]{:S(2)}) copy-start(f32[3,128,2048]{1,2,0:T(8,128)} %copy-done.1) | copy-start | bytes 9437188
  125.5 59.8 %copy-start.8 = (f32[2048]{0:T(1024)S(1)}, f32[2048]{0:T(1024)}, u32[]{:S(2)}) copy-start(f32[2048]{0:T(1024)} %param.17) | copy-start | bytes 24580
where the time goes:
time: 190 us; the launch traced here: 187 us
  blocking collectives  59.1 us (31%)
  matrix products  52.5 us (28%)
  waiting for transfers between devices  28.9 us (15%)
  starting transfers between devices  20.5 us (11%)
  other arithmetic  17 us (9%)
  local copies, waits for them, and re-layouts  8.18 us (4%)
    all_to_all x1, blocking collectives, body(): lax.all_to_all(conv_cols, 'ctx', split_axis=1, concat_axis=0, tiled=True)  59.1 us
    dot_general x12, matrix products, section_inner(): jnp.einsum('ckb,bj->ckj', data, table, precision=HIGHEST, preferred_eleme...  29.7 us
    all_to_all x1, waiting for transfers between devices, body(): lax.all_to_all(driven.T, 'ctx', split_axis=0, concat_axis=1, tiled=True)  28.9 us
    all_to_all x1, starting transfers between devices, body(): lax.all_to_all(driven.T, 'ctx', split_axis=0, concat_axis=1, tiled=True)  15.5 us
    add x1, other arithmetic, body(): short_out + short_weight[tap_index][:, None, :] * extended[:, offset:offs...  13.3 us
    dot_general x6, matrix products, section_outer(): jnp.einsum('ka,cab->ckb', table, data, precision=HIGHEST, preferred_eleme...  12.8 us
    ppermute x1, starting transfers between devices, shifted(): return lax.ppermute(x, axis, pairs)  4.94 us
    dot_general x1, matrix products, filter_rows(): jnp.dot(inputs, pos_in, precision=HIGHEST, preferred_element_type=jnp.flo...  4.39 us
  transfers between devices with their start and end apart: 2, of which 1 were waited for; matrix products, arithmetic and copies ran while one was open for 16% of the time, Pallas kernels for 0%

commit v1 on v0

v1 whole, which is shorter than its diff:
```python
import math

import jax
import jax.numpy as jnp
import numpy as np
from jax import lax
from jax.experimental import pallas as pl
from jax.experimental.pallas import tpu as pltpu
from jax.sharding import PartitionSpec as P

BANDS = 16
TAPS = 7
LANES = 128
EDGE = 8
CHUNKS = 2
HIGHEST = lax.Precision.HIGHEST
MESH = pl.DeviceIdType.MESH

OUT_POWER = 12
BACK_POWER = 10
OUT_SPAN = 248.0 / OUT_POWER
BACK_SPAN = 248.0 / BACK_POWER
OUT_LOW = 2.0 ** (-OUT_SPAN / 2)
BACK_LOW = 2.0 ** (-BACK_SPAN / 2)
OUT_REACH = (2.0**OUT_SPAN - 1.0) * OUT_LOW
BACK_REACH = (2.0**BACK_SPAN - 1.0) * BACK_LOW
LARGEST = 6.0


def position_table(total_len, rows):
    positions = np.arange(total_len, dtype=np.float32)
    bands = np.arange(1, BANDS + 1, dtype=np.float32)
    angles = positions[None, :] * bands[:, None] * np.float32(2.0 * math.pi / total_len)
    angles = angles.astype(np.float32).astype(np.float64)
    table = np.zeros((rows, total_len), np.float32)
    table[0] = positions / np.float32(total_len)
    table[1 : 1 + BANDS] = np.cos(angles)
    table[1 + BANDS : 1 + 2 * BANDS] = np.sin(angles)
    table[1 + 2 * BANDS] = 1.0
    return table


def two_parts(table):
    high = table.astype(jnp.bfloat16)
    low = (table - high.astype(np.float64)).astype(jnp.bfloat16)
    return high, low


def inner_tables():
    ids = np.arange(LANES, dtype=np.float64)
    angles = 2.0 * math.pi / LANES * np.mod(ids[:, None] * ids[None, :], LANES)
    cos, sin = np.cos(angles), np.sin(angles)
    forth = np.block([[cos, -sin], [sin, cos]])
    back = np.block([[cos, sin], [-sin, cos]])
    return np.stack(two_parts(forth) + two_parts(back))


def twist_table(outer, total_len):
    angles = (
        2.0
        * math.pi
        / total_len
        * (np.arange(outer)[:, None] + 0.25)
        * np.arange(LANES)[None, :]
    )
    return np.stack([np.cos(angles), np.sin(angles)], axis=1).astype(np.float32)


def turned(real, imag, cos, sin):
    if abs(sin) < 1e-12 and cos > 0:
        return real, imag
    if abs(cos) < 1e-12:
        return (-imag, real) if sin > 0 else (imag, -real)
    if abs(abs(cos) - abs(sin)) < 1e-12 and cos > 0:
        half = math.sqrt(0.5)
        if sin > 0:
            return (real - imag) * half, (real + imag) * half
        return (real + imag) * half, (imag - real) * half
    return real * cos - imag * sin, real * sin + imag * cos


def short_fourier(items, sign):
    size = len(items)
    if size == 1:
        return items
    even = short_fourier(items[0::2], sign)
    odd = short_fourier(items[1::2], sign)
    first, second = [], []
    for at in range(size // 2):
        angle = sign * 2.0 * math.pi * at / size
        real, imag = turned(odd[at][0], odd[at][1], math.cos(angle), math.sin(angle))
        first.append((even[at][0] + real, even[at][1] + imag))
        second.append((even[at][0] - real, even[at][1] - imag))
    return first + second


def sine(x):
    turns = jnp.round(x * (1.0 / math.pi))
    r = x - turns * 3.140625
    r = r - turns * 9.67502593994140625e-4
    r = r - turns * 1.509957990978376432e-7
    s = r * r
    poly = -2.38898859e-8 * s + 2.75255613e-6
    poly = poly * s - 1.98408743e-4
    poly = poly * s + 8.33333310e-3
    poly = poly * s - 1.66666667e-1
    value = r + r * s * poly
    half = turns * 0.5
    odd = half - jnp.floor(half)
    return value * (1.0 - 4.0 * odd)


def coded(value, scale, low, power):
    w = low + jnp.abs(value) * scale
    two = w * w
    four = two * two
    eight = four * four
    if power == 12:
        top = eight * four
    else:
        top = eight * two
    return jnp.where(value < 0, -top, top)


def decoded(code, low, power):
    w = jnp.exp(jnp.log(jnp.abs(code)) * (1.0 / power)) - low
    return jnp.where(code < 0, -w, w)


def kernel(
    ctx,
    proj_any,
    weight_any,
    *refs,
):
    (
        pos_in_any,
        pos_bias_any,
        sine_freq_any,
        pos_mid_any,
        pos_out_any,
        decay_any,
        skip_any,
        feats_any,
        inner_any,
        twist_any,
        out,
        proj,
        weight,
        pos_in,
        pos_bias,
        sine_freq,
        pos_mid,
        pos_out,
        decay,
        skip,
        feats,
        inner,
        twist,
        wide,
        driven,
        rim,
        first_w,
        second_w,
        second,
        own_out,
        own_decay,
        values,
        spec,
        filt,
        send_f,
        got_f,
        send_r,
        got_r,
        local_sem,
        rim_send,
        rim_recv,
        f_send,
        f_recv,
        r_send,
        r_recv,
    ) = refs
    me = lax.axis_index("ctx")
    chip = lax.div(me, 2)
    core = lax.rem(me, 2)
    chips = ctx // 2
    rows = proj.shape[1]
    own = got_f.shape[2]
    total_len = ctx * rows

    early = ((weight_any, weight), (proj_any, proj))
    late = (
        (pos_in_any, pos_in),
        (pos_bias_any, pos_bias),
        (sine_freq_any, sine_freq),
        (pos_mid_any, pos_mid),
        (pos_out_any, pos_out),
        (decay_any, decay),
        (skip_any, skip),
        (feats_any, feats),
        (inner_any, inner),
        (twist_any, twist),
    )
    fetches = [
        pltpu.make_async_copy(there, here, local_sem.at[i])
        for i, (there, here) in enumerate(early + late)
    ]
    for fetch in fetches:
        fetch.start()

    barrier = pltpu.get_barrier_semaphore()

    def greet(i, carry):
        pl.semaphore_signal(
            barrier, inc=1, device_id={"ctx": lax.rem(me + i, ctx)}, device_id_type=MESH
        )
        return carry

    lax.fori_loop(1, ctx, greet, 0)

    def slab(n):
        return pl.ds(pl.multiple_of(n * LANES, LANES), LANES)

    def taps_sum(stream, n, start, count):
        total = None
        for tap in range(TAPS):
            part = weight[stream, pl.ds(tap, 1), slab(n)] * wide[
                stream, n, EDGE + start - tap : EDGE + start - tap + count, :
            ]
            total = part if total is None else total + part
        return total

    for fetch in fetches[: len(early)]:
        fetch.wait()

    def widen(n, carry):
        for stream in range(3):
            wide[stream, n, EDGE : EDGE + rows, :] = proj[stream, :, slab(n)].astype(jnp.float32)
        driven[n, EDGE:rows, :] = taps_sum(0, n, EDGE, rows - EDGE) * taps_sum(
            2, n, EDGE, rows - EDGE
        )
        return carry

    lax.fori_loop(0, chips, widen, 0)

    pl.semaphore_wait(barrier, ctx - 1)

    rim_copy = pltpu.make_async_remote_copy(
        src_ref=proj.at[:, pl.ds(rows - EDGE, EDGE), :],
        dst_ref=rim,
        send_sem=rim_send,
        recv_sem=rim_recv,
        device_id={"ctx": lax.rem(me + 1, ctx)},
        device_id_type=MESH,
    )

    @pl.when(me < ctx - 1)
    def _():
        rim_copy.start()

    @pl.when(me == 0)
    def _():
        rim[...] = jnp.zeros_like(rim)

    @pl.when(me > 0)
    def _():
        rim_copy.wait_recv()

    def forth(g, to):
        return pltpu.make_async_remote_copy(
            src_ref=send_f.at[g, to],
            dst_ref=got_f.at[g, me],
            send_sem=f_send.at[g],
            recv_sem=f_recv.at[g, me],
            device_id={"ctx": to},
            device_id_type=MESH,
        )

    def back(g, to):
        return pltpu.make_async_remote_copy(
            src_ref=send_r.at[g, to],
            dst_ref=got_r.at[g, me],
            send_sem=r_send.at[g],
            recv_sem=r_recv.at[g, me],
            device_id={"ctx": to},
            device_id_type=MESH,
        )

    def to_chip(i):
        far = chips // 2 - lax.div(i + 1, 2)
        away = jnp.where(lax.rem(i, 2) == 1, far, chips - far)
        return lax.rem(chip + away, chips)

    def bound(n):
        total = 1.0
        for stream in (0, 2):
            size = None
            for tap in range(TAPS):
                part = jnp.abs(weight[stream, pl.ds(tap, 1), slab(n)])
                size = part if size is None else size + part
            total = total * (size * LARGEST)
        return jnp.maximum(total, 1e-30)

    def push(make, g, n):
        for c in range(2):
            to = 2 * n + c

            @pl.when(to != me)
            def _():
                make(g, to).start()

    def encode(i, carry):
        n = to_chip(i)
        for stream in range(3):
            wide[stream, n, 0:EDGE, :] = rim[stream, :, slab(n)].astype(jnp.float32)
        driven[n, 0:EDGE, :] = taps_sum(0, n, 0, EDGE) * taps_sum(2, n, 0, EDGE)
        code = coded(driven[n], OUT_REACH / bound(n), OUT_LOW, OUT_POWER)
        code = code.T.astype(jnp.bfloat16)
        for c in range(2):
            for g in range(CHUNKS):
                low = (c * CHUNKS + g) * own
                send_f[g, 2 * n + c] = code[low : low + own]
        push(forth, 0, n)
        return carry

    lax.fori_loop(0, chips, encode, 0)

    def rest(g, make):
        def step(i, carry):
            push(make, g, to_chip(i))
            return carry

        lax.fori_loop(0, chips, step, 0)

    for g in range(1, CHUNKS):
        rest(g, forth)
    for g in range(CHUNKS):
        got_f[g, me] = send_f[g, me]

    for fetch in fetches[len(early) :]:
        fetch.wait()
    taps_in = pos_in.shape[0]
    freq = sine_freq[...]
    first_w[...] = jnp.zeros_like(first_w)
    first_w[0:taps_in, :] = pos_in[...] * freq
    first_w[taps_in : taps_in + 1, :] = pos_bias[...] * freq
    second_w[...] = pos_mid[...] * freq
    turn = (((0,), (0,)), ((), ()))
    span = 512

    def network(j, carry):
        at = pl.ds(pl.multiple_of(j * span, span), span)
        one = sine(
            lax.dot_general(
                first_w[...],
                feats[:, at],
                turn,
                precision=HIGHEST,
                preferred_element_type=jnp.float32,
            )
        )
        second[:, at] = sine(
            lax.dot_general(
                second_w[...], one, turn, precision=HIGHEST, preferred_element_type=jnp.float32
            )
        )
        return carry

    lax.fori_loop(0, total_len // span, network, 0)
    own_out[...] = pos_out[:, slab(chip)].T
    own_decay[...] = jnp.broadcast_to(decay[:, slab(chip)], (LANES, LANES)).T

    group = 8

    def halves(x):
        high = x.astype(jnp.bfloat16)
        return high, (x - high.astype(jnp.float32)).astype(jnp.bfloat16)

    def product(x, which):
        high, low = halves(x)
        return (
            jnp.dot(high, inner[which], preferred_element_type=jnp.float32)
            + jnp.dot(low, inner[which], preferred_element_type=jnp.float32)
            + jnp.dot(high, inner[which + 1], preferred_element_type=jnp.float32)
        )

    def outer_forth():
        def step(j, carry):
            at = pl.ds(pl.multiple_of(j * group, group), group)
            items = []
            for a in range(ctx):
                x = values[a, at, :]
                angle = 2.0 * math.pi * a / (4 * ctx)
                items.append((x * math.cos(angle), x * -math.sin(angle)))
            for k, (real, imag) in enumerate(short_fourier(items, -1)):
                cos, sin = twist[k, 0:1, :], twist[k, 1:2, :]
                spec[k, at, 0:LANES] = real * cos + imag * sin
                spec[k, at, LANES : 2 * LANES] = imag * cos - real * sin
            return carry

        lax.fori_loop(0, own // group, step, 0)

    def outer_back():
        def step(j, carry):
            at = pl.ds(pl.multiple_of(j * group, group), group)
            items = []
            for k in range(ctx):
                real, imag = spec[k, at, 0:LANES], spec[k, at, LANES : 2 * LANES]
                cos, sin = twist[k, 0:1, :], twist[k, 1:2, :]
                items.append((real * cos - imag * sin, imag * cos + real * sin))
            for a, (real, imag) in enumerate(short_fourier(items, 1)):
                angle = 2.0 * math.pi * a / (4 * ctx)
                values[a, at, :] = real * math.cos(angle) - imag * math.sin(angle)
            return carry

        lax.fori_loop(0, own // group, step, 0)

    for g in range(CHUNKS):
        low = pl.ds(pl.multiple_of(core * (CHUNKS * own) + g * own, own), own)
        out_rows = own_out[low, :]
        out_high, out_low = halves(out_rows)
        rate = own_decay[low, :]

        def fill(a, squares):
            at = slab(a)
            high, less = halves(second[:, at])
            raw = (
                jnp.dot(out_high, high, preferred_element_type=jnp.float32)
                + jnp.dot(out_low, high, preferred_element_type=jnp.float32)
                + jnp.dot(out_high, less, preferred_element_type=jnp.float32)
            )
            place = lax.broadcasted_iota(jnp.int32, (own, LANES), 1) + a * LANES
            long_filter = raw * jnp.exp(-(rate * place.astype(jnp.float32)))
            values[a] = long_filter
            return squares + long_filter * long_filter

        squares = lax.fori_loop(0, ctx, fill, jnp.zeros((own, LANES), jnp.float32))
        norm = jnp.sqrt(jnp.sum(squares, axis=1, keepdims=True) + 1e-05)
        scale = (1.0 / total_len) / norm
        outer_forth()
        full = product(spec[...].reshape(ctx * own, 2 * LANES), 0)
        filt[g] = full.reshape(ctx, own, 2 * LANES) * scale[None]

    for g in range(CHUNKS):

        def arrive(i, carry):
            frm = lax.rem(me + i, ctx)
            pltpu.make_async_remote_copy(
                src_ref=send_f.at[g, frm],
                dst_ref=got_f.at[g, frm],
                send_sem=f_send.at[g],
                recv_sem=f_recv.at[g, frm],
                device_id={"ctx": frm},
                device_id_type=MESH,
            ).wait_recv()
            return carry

        lax.fori_loop(1, ctx, arrive, 0)

        def decode(a, carry):
            values[a] = decoded(got_f[g, a].astype(jnp.float32), OUT_LOW, OUT_POWER)
            return carry

        lax.fori_loop(0, ctx, decode, 0)
        outer_forth()
        full = product(spec[...].reshape(ctx * own, 2 * LANES), 0)
        real, imag = full[:, :LANES], full[:, LANES:]
        response = filt[g].reshape(ctx * own, 2 * LANES)
        f_real, f_imag = response[:, :LANES], response[:, LANES:]
        mixed_real = real * f_real - imag * f_imag
        mixed_imag = real * f_imag + imag * f_real
        full = product(jnp.concatenate([mixed_real, mixed_imag], axis=1), 2)
        spec[...] = full.reshape(ctx, own, 2 * LANES)
        outer_back()

        def pack(i, carry):
            n = to_chip(i)
            for c in range(2):
                a = 2 * n + c
                code = coded(values[a], BACK_REACH / (64.0 * OUT_REACH), BACK_LOW, BACK_POWER)
                send_r[g, a] = code.astype(jnp.bfloat16)
            push(back, g, n)
            return carry

        lax.fori_loop(0, chips, pack, 0)
        got_r[g, me] = send_r[g, me]

    def gate(n, carry):
        wide[1, n, EDGE : EDGE + rows, :] = taps_sum(1, n, 0, rows)
        return carry

    lax.fori_loop(0, chips, gate, 0)

    def finish(i, carry):
        n = to_chip(chips - 1 - i)
        parts = []
        for c in range(2):
            frm = 2 * n + c
            for g in range(CHUNKS):

                @pl.when(frm != me)
                def _():
                    pltpu.make_async_remote_copy(
                        src_ref=send_r.at[g, frm],
                        dst_ref=got_r.at[g, frm],
                        send_sem=r_send.at[g],
                        recv_sem=r_recv.at[g, frm],
                        device_id={"ctx": frm},
                        device_id_type=MESH,
                    ).wait_recv()

        for c in range(2):
            for g in range(CHUNKS):
                parts.append(got_r[g, 2 * n + c].astype(jnp.float32))
        code = jnp.concatenate(parts, axis=0).T
        unit = bound(n) * (64.0 / BACK_REACH)
        long_conv = decoded(code, BACK_LOW, BACK_POWER) * unit
        right = wide[1, n, EDGE : EDGE + rows, :]
        mixed = right * (long_conv + skip[:, slab(n)] * driven[n])
        out[:, slab(n)] = mixed.astype(jnp.bfloat16)
        return carry

    lax.fori_loop(0, chips, finish, 0)

    @pl.when(me < ctx - 1)
    def _():
        rim_copy.wait_send()

    for g in range(CHUNKS):
        for buffer, sem in ((send_f, f_send), (send_r, r_send)):
            sent = buffer.at[g, pl.ds(0, ctx - 1)]
            pltpu.make_async_remote_copy(
                src_ref=sent,
                dst_ref=sent,
                send_sem=sem.at[g],
                recv_sem=sem.at[g],
                device_id={"ctx": me},
                device_id_type=MESH,
            ).wait_send()


def body(
    projected, short_weight, pos_in, pos_bias, sine_freq, pos_mid, pos_out, decay_rate, skip_gain
):
    ctx = lax.axis_size("ctx")
    _, rows, width = projected.shape
    own = width // ctx // CHUNKS
    order = pos_mid.shape[0]
    total_len = ctx * rows
    feat_rows = -(-(pos_in.shape[0] + 1) // 8) * 8
    feats = jnp.asarray(position_table(total_len, feat_rows))
    inner = jnp.asarray(inner_tables())
    twist = jnp.asarray(twist_table(ctx, total_len))
    vmem = pl.BlockSpec(memory_space=pltpu.VMEM)
    left = pl.BlockSpec(memory_space=pltpu.HBM)
    bf16, f32 = jnp.bfloat16, jnp.float32
    dma = pltpu.SemaphoreType.DMA
    wires = [pltpu.VMEM((CHUNKS, ctx, own, rows), bf16)] * 4

    def call(*refs):
        return kernel(ctx, *refs)

    operands = (
        projected,
        short_weight.transpose(1, 0, 2),
        pos_in,
        pos_bias.reshape(1, -1),
        sine_freq.reshape(1, -1),
        pos_mid,
        pos_out,
        decay_rate.reshape(1, -1),
        skip_gain.reshape(1, -1),
        feats,
        inner,
        twist,
    )
    return pl.pallas_call(
        call,
        out_shape=jax.ShapeDtypeStruct((rows, width), bf16),
        in_specs=[left] * 12,
        out_specs=vmem,
        scratch_shapes=[
            *[pltpu.VMEM(operand.shape, operand.dtype) for operand in operands],
            pltpu.VMEM((3, width // LANES, EDGE + rows, LANES), f32),
            pltpu.VMEM((width // LANES, rows, LANES), f32),
            pltpu.VMEM((3, EDGE, width), bf16),
            pltpu.VMEM((feat_rows, order), f32),
            pltpu.VMEM((order, order), f32),
            pltpu.VMEM((order, total_len), f32),
            pltpu.VMEM((LANES, order), f32),
            pltpu.VMEM((LANES, LANES), f32),
            pltpu.VMEM((ctx, own, LANES), f32),
            pltpu.VMEM((ctx, own, 2 * LANES), f32),
            pltpu.VMEM((CHUNKS, ctx, own, 2 * LANES), f32),
            *wires,
            dma((len(operands),)),
            dma,
            dma,
            dma((CHUNKS,)),
            dma((CHUNKS, ctx)),
            dma((CHUNKS,)),
            dma((CHUNKS, ctx)),
        ],
        compiler_params=pltpu.CompilerParams(
            collective_id=0, has_side_effects=True, vmem_limit_bytes=60 * 1024 * 1024
        ),
        name="hyena",
    )(*operands)


def solution(mesh):
    placed = (
        P(None, ("dp", "ctx"), "chan"),
        P(None, None, "chan"),
        P(),
        P(),
        P(),
        P(),
        P(None, "chan"),
        P("chan"),
        P("chan"),
    )
    return jax.shard_map(
        body, mesh=mesh, in_specs=placed, out_specs=P(("dp", "ctx"), "chan"), check_vma=False
    )
```

time: 190 us -> 71.3 us (0.38); the launches traced: 187 us -> 71.2 us
  Pallas kernels: 0 us -> 69.3 us
  blocking collectives: 59.1 us -> 0 us
  matrix products: 52.5 us -> 0 us
  waiting for transfers between devices: 28.9 us -> 0 us
  starting transfers between devices: 20.5 us -> 0 us
  other arithmetic: 17 us -> 0 us
  local copies, waits for them, and re-layouts: 8.18 us -> 1.88 us
    pallas_call x0 -> x1, Pallas kernels: none -> 69.3 us  [body(): pl.pallas_call(call, out_shape=jax.ShapeDtypeStruct((rows, width), bf16),...]
    all_to_all x1 -> x0, blocking collectives: 59.1 us -> none  [body(): lax.all_to_all(conv_cols, 'ctx', split_axis=1, concat_axis=0, tiled=True)]
    dot_general x21 -> x0, matrix products: 52.5 us -> none  [the longest x12 29.7 us: section_inner(): jnp.einsum('ckb,bj->ckj', data, table, precision=HIGHEST, preferred_eleme...]
    all_to_all x1 -> x0, waiting for transfers between devices: 28.9 us -> none  [body(): lax.all_to_all(driven.T, 'ctx', split_axis=0, concat_axis=1, tiled=True)]
    all_to_all x1 -> x0, starting transfers between devices: 15.5 us -> none  [body(): lax.all_to_all(driven.T, 'ctx', split_axis=0, concat_axis=1, tiled=True)]
    add x2 -> x0, other arithmetic: 13.4 us -> none  [the longest x1 13.3 us: body(): short_out + short_weight[tap_index][:, None, :] * extended[:, offset:offs...]
    ppermute x1 -> x0, starting transfers between devices: 4.94 us -> none  [shifted(): return lax.ppermute(x, axis, pairs)]
    unnamed x28 -> x1, local copies, waits for them, and re-layouts: 3.87 us -> 1.88 us
  transfers between devices with their start and end apart: 2 -> 0, of which waited for: 1 -> 0; matrix products, arithmetic and copies ran while one was open for 16% -> 0% of each run, Pallas kernels for 0% -> 0%
where the time goes in v1:
time: 71.3 us; the launch traced here: 71.2 us
  Pallas kernels  69.3 us (97%)
  local copies, waits for them, and re-layouts  1.88 us (3%)
    pallas_call x1, Pallas kernels, body(): pl.pallas_call(call, out_shape=jax.ShapeDtypeStruct((rows, width), bf16),...  69.3 us
    unnamed x1, local copies, waits for them, and re-layouts  1.88 us

profile of v1, /device:TPU:1, one launch (start us, length us, event | category | flops | bytes accessed | tf_op | source)
XLA Modules:
  0.0 71.2 jit_solution(12552162289020738322)
XLA Ops:
  0.0 69.3 %hyena.1 = bf16[128,2048]{1,0:T(8,128)(2,1)} custom-call(bf16[3,128,2048]{2,1,0:T(8,128)(2,1)} %refs_0_.1, f32[3,7,2048]{2,1,0:T(8,128)} %bitcast.5, f32[33,64]{1,0:T(8,128)} %refs_2_.1, f32[1,64]{1,0:T(1,128)} %bitcast.8, f32[1,64]{1,0:T(1,128)} %bitcast.9, f32[64,64]{1,0:T(8,128)} %refs_5_.1, f32[64,2048]{1,0:T(8,128)} %refs_6_.1, f32[1,2048]{1,0:T(1,128)} %bitcast.6, ...), custom_call_target="tpu_custom_call" | custom-call | tf_op jit(solution)/shard_map/hyena/pallas_call | solution.py:577
  69.3 1.9 %copy.14 = bf16[128,2048]{1,0:T(8,128)(2,1)} copy(bf16[128,2048]{1,0:T(8,128)(2,1)} %hyena.1) | data formatting | bytes 1048576

commit v2 on v1

--- a/solution.py
+++ b/solution.py
@@ -13,7 +13,6 @@
 LANES = 128
 EDGE = 8
 CHUNKS = 2
-HIGHEST = lax.Precision.HIGHEST
 MESH = pl.DeviceIdType.MESH
 
 OUT_POWER = 12
@@ -44,6 +43,22 @@
     high = table.astype(jnp.bfloat16)
     low = (table - high.astype(np.float64)).astype(jnp.bfloat16)
     return high, low
+
+
+LEFT_PARTS = (0, 0, 1, 0, 1, 2)
+RIGHT_PARTS = (0, 1, 0, 2, 1, 0)
+
+
+def stacked_positions(total_len, rows, depth):
+    table = position_table(total_len, rows).astype(np.float64)
+    parts = []
+    for _ in range(3):
+        part = table.astype(jnp.bfloat16)
+        parts.append(part)
+        table = table - part.astype(np.float64)
+    stack = np.concatenate([parts[at] for at in RIGHT_PARTS])
+    empty = np.zeros((depth - stack.shape[0], total_len), jnp.bfloat16)
+    return np.concatenate([stack, empty])
 
 
 def inner_tables():
@@ -129,6 +144,7 @@
 
 def kernel(
     ctx,
+    feat_rows,
     proj_any,
     weight_any,
     *refs,
@@ -162,10 +178,13 @@
         rim,
         first_w,
         second_w,
-        second,
-        own_out,
+        third_w,
+        first_t,
+        second_t,
+        third_t,
         own_decay,
         values,
+        taps,
         spec,
         filt,
         send_f,
@@ -179,6 +198,7 @@
         f_recv,
         r_send,
         r_recv,
+        news,
     ) = refs
     me = lax.axis_index("ctx")
     chip = lax.div(me, 2)
@@ -205,18 +225,20 @@
         pltpu.make_async_copy(there, here, local_sem.at[i])
         for i, (there, here) in enumerate(early + late)
     ]
-    for fetch in fetches:
+    for fetch in fetches[: len(early)]:
         fetch.start()
 
     barrier = pltpu.get_barrier_semaphore()
 
-    def greet(i, carry):
-        pl.semaphore_signal(
-            barrier, inc=1, device_id={"ctx": lax.rem(me + i, ctx)}, device_id_type=MESH
-        )
-        return carry
-
-    lax.fori_loop(1, ctx, greet, 0)
+    right = lax.rem(chip + 1, chips)
+    left = lax.rem(chip + chips - 1, chips)
+
+    def tell(sem, to):
+        pl.semaphore_signal(sem, inc=1, device_id={"ctx": to}, device_id_type=MESH)
+
+    near = (2 * chip + 1 - core, 2 * left, 2 * left + 1, 2 * right, 2 * right + 1)
+    for to in near:
+        tell(barrier, to)
 
     def slab(n):
         return pl.ds(pl.multiple_of(n * LANES, LANES), LANES)
@@ -230,8 +252,36 @@
             total = part if total is None else total + part
         return total
 
+    pl.semaphore_wait(barrier, len(near))
+
+    rim_copy = pltpu.make_async_remote_copy(
+        src_ref=proj_any.at[:, pl.ds(rows - EDGE, EDGE), :],
+        dst_ref=rim,
+        send_sem=rim_send,
+        recv_sem=rim_recv,
+        device_id={"ctx": lax.rem(me + 1, ctx)},
+        device_id_type=MESH,
+    )
+
+    def spread(step):
+        away = 2**step
+        tell(news.at[step, 0], 2 * lax.rem(chip + away, chips) + core)
+        tell(news.at[step, 1], 2 * lax.rem(chip + chips - away, chips) + core)
+
+    def hear(step):
+        for side in range(2):
+            pl.semaphore_wait(news.at[step, side], 1)
+
+    spread(0)
+
+    @pl.when(me < ctx - 1)
+    def _():
+        rim_copy.start()
+
     for fetch in fetches[: len(early)]:
         fetch.wait()
+    for fetch in fetches[len(early) :]:
+        fetch.start()
 
     def widen(n, carry):
         for stream in range(3):
@@ -241,22 +291,12 @@
         )
         return carry
 
-    lax.fori_loop(0, chips, widen, 0)
-
-    pl.semaphore_wait(barrier, ctx - 1)
-
-    rim_copy = pltpu.make_async_remote_copy(
-        src_ref=proj.at[:, pl.ds(rows - EDGE, EDGE), :],
-        dst_ref=rim,
-        send_sem=rim_send,
-        recv_sem=rim_recv,
-        device_id={"ctx": lax.rem(me + 1, ctx)},
-        device_id_type=MESH,
-    )
-
-    @pl.when(me < ctx - 1)
-    def _():
-        rim_copy.start()
+    lax.fori_loop(0, chips // 2, widen, 0)
+    hear(0)
+    spread(1)
+    lax.fori_loop(chips // 2, chips, widen, 0)
+    hear(1)
+    spread(2)
 
     @pl.when(me == 0)
     def _():
@@ -309,8 +349,7 @@
             def _():
                 make(g, to).start()
 
-    def encode(i, carry):
-        n = to_chip(i)
+    def encode(n):
         for stream in range(3):
             wide[stream, n, 0:EDGE, :] = rim[stream, :, slab(n)].astype(jnp.float32)
         driven[n, 0:EDGE, :] = taps_sum(0, n, 0, EDGE) * taps_sum(2, n, 0, EDGE)
@@ -321,9 +360,22 @@
                 low = (c * CHUNKS + g) * own
                 send_f[g, 2 * n + c] = code[low : low + own]
         push(forth, 0, n)
-        return carry
-
-    lax.fori_loop(0, chips, encode, 0)
+
+    def around(first):
+        def step(i, carry):
+            away = first - lax.div(i, 2)
+            away = jnp.where(lax.rem(i, 2) == 0, away, chips - away)
+            encode(lax.rem(chip + away, chips))
+            return carry
+
+        return step
+
+    quarter = chips // 4
+    lax.fori_loop(0, 2 * quarter, around(quarter), 0)
+    encode(chip)
+    hear(2)
+    encode(lax.rem(chip + 2 * quarter, chips))
+    lax.fori_loop(0, 2 * quarter - 2, around(2 * quarter - 1), 0)
 
     def rest(g, make):
         def step(i, carry):
@@ -340,41 +392,68 @@
     for fetch in fetches[len(early) :]:
         fetch.wait()
     taps_in = pos_in.shape[0]
+    order = pos_mid.shape[0]
     freq = sine_freq[...]
-    first_w[...] = jnp.zeros_like(first_w)
-    first_w[0:taps_in, :] = pos_in[...] * freq
-    first_w[taps_in : taps_in + 1, :] = pos_bias[...] * freq
-    second_w[...] = pos_mid[...] * freq
-    turn = (((0,), (0,)), ((), ()))
-    span = 512
-
-    def network(j, carry):
-        at = pl.ds(pl.multiple_of(j * span, span), span)
-        one = sine(
-            lax.dot_general(
-                first_w[...],
-                feats[:, at],
-                turn,
-                precision=HIGHEST,
-                preferred_element_type=jnp.float32,
-            )
-        )
-        second[:, at] = sine(
-            lax.dot_general(
-                second_w[...], one, turn, precision=HIGHEST, preferred_element_type=jnp.float32
-            )
-        )
-        return carry
-
-    lax.fori_loop(0, total_len // span, network, 0)
-    own_out[...] = pos_out[:, slab(chip)].T
-    own_decay[...] = jnp.broadcast_to(decay[:, slab(chip)], (LANES, LANES)).T
-
-    group = 8
 
     def halves(x):
         high = x.astype(jnp.bfloat16)
         return high, (x - high.astype(jnp.float32)).astype(jnp.bfloat16)
+
+    def thirds(x):
+        high, low = halves(x)
+        rest_of = x - high.astype(jnp.float32)
+        return high, low, (rest_of - low.astype(jnp.float32)).astype(jnp.bfloat16)
+
+    first_w[...] = jnp.zeros_like(first_w)
+    second_w[...] = jnp.zeros_like(second_w)
+    third_w[...] = jnp.zeros_like(third_w)
+    entry = thirds(pos_in[...] * freq)
+    offset = thirds(pos_bias[...] * freq)
+    middle = thirds(pos_mid[...] * freq)
+    exit_high, exit_low = halves(pos_out[:, slab(chip)])
+    for i, part in enumerate(LEFT_PARTS):
+        at = i * feat_rows
+        first_w[at : at + taps_in, 0:order] = entry[part].astype(jnp.float32)
+        first_w[at + taps_in : at + taps_in + 1, 0:order] = offset[part].astype(jnp.float32)
+        second_w[i * order : (i + 1) * order, 0:order] = middle[part].astype(jnp.float32)
+    for i, part in enumerate((exit_high, exit_low, exit_high)):
+        third_w[i * order : (i + 1) * order, :] = part.astype(jnp.float32)
+    first_t[...] = first_w[...].T[0:order].astype(jnp.bfloat16)
+    second_t[...] = second_w[...].T[0:order].astype(jnp.bfloat16)
+    third_t[...] = third_w[...].T
+    own_decay[...] = jnp.broadcast_to(decay[:, slab(chip)], (LANES, LANES)).T
+
+    mine = pl.ds(pl.multiple_of(core * (CHUNKS * own), CHUNKS * own), CHUNKS * own)
+    third = third_t[mine, :].astype(jnp.bfloat16)
+    rate = own_decay[mine, :]
+    span = 512
+
+    def network(j, squares):
+        at = pl.ds(pl.multiple_of(j * span, span), span)
+        one = thirds(sine(jnp.dot(first_t[...], feats[:, at], preferred_element_type=jnp.float32)))
+        one = jnp.concatenate([one[part] for part in RIGHT_PARTS], axis=0)
+        two = sine(jnp.dot(second_t[...], one, preferred_element_type=jnp.float32))
+        high, low = halves(two)
+        two = jnp.concatenate([high, high, low], axis=0)
+        raw = jnp.dot(third, two, preferred_element_type=jnp.float32)
+        for i in range(span // LANES):
+            a = j * (span // LANES) + i
+            place = lax.broadcasted_iota(jnp.int32, (CHUNKS * own, LANES), 1) + a * LANES
+            long_filter = raw[:, i * LANES : (i + 1) * LANES] * jnp.exp(
+                -(rate * place.astype(jnp.float32))
+            )
+            for g in range(CHUNKS):
+                taps[g, a] = long_filter[g * own : (g + 1) * own]
+            squares = squares + long_filter * long_filter
+        return squares
+
+    squares = lax.fori_loop(
+        0, total_len // span, network, jnp.zeros((CHUNKS * own, LANES), jnp.float32)
+    )
+    norm = jnp.sqrt(jnp.sum(squares, axis=1, keepdims=True) + 1e-05)
+    scale = (1.0 / total_len) / norm
+
+    group = 8
 
     def product(x, which):
         high, low = halves(x)
@@ -384,12 +463,12 @@
             + jnp.dot(high, inner[which + 1], preferred_element_type=jnp.float32)
         )
 
-    def outer_forth():
+    def outer_forth(source):
         def step(j, carry):
             at = pl.ds(pl.multiple_of(j * group, group), group)
             items = []
             for a in range(ctx):
-                x = values[a, at, :]
+                x = source[a, at, :]
                 angle = 2.0 * math.pi * a / (4 * ctx)
                 items.append((x * math.cos(angle), x * -math.sin(angle)))
             for k, (real, imag) in enumerate(short_fourier(items, -1)):
@@ -416,30 +495,9 @@
         lax.fori_loop(0, own // group, step, 0)
 
     for g in range(CHUNKS):
-        low = pl.ds(pl.multiple_of(core * (CHUNKS * own) + g * own, own), own)
-        out_rows = own_out[low, :]
-        out_high, out_low = halves(out_rows)
-        rate = own_decay[low, :]
-
-        def fill(a, squares):
-            at = slab(a)
-            high, less = halves(second[:, at])
-            raw = (
-                jnp.dot(out_high, high, preferred_element_type=jnp.float32)
-                + jnp.dot(out_low, high, preferred_element_type=jnp.float32)
-                + jnp.dot(out_high, less, preferred_element_type=jnp.float32)
-            )
-            place = lax.broadcasted_iota(jnp.int32, (own, LANES), 1) + a * LANES
-            long_filter = raw * jnp.exp(-(rate * place.astype(jnp.float32)))
-            values[a] = long_filter
-            return squares + long_filter * long_filter
-
-        squares = lax.fori_loop(0, ctx, fill, jnp.zeros((own, LANES), jnp.float32))
-        norm = jnp.sqrt(jnp.sum(squares, axis=1, keepdims=True) + 1e-05)
-        scale = (1.0 / total_len) / norm
-        outer_forth()
+        outer_forth(taps.at[g])
         full = product(spec[...].reshape(ctx * own, 2 * LANES), 0)
-        filt[g] = full.reshape(ctx, own, 2 * LANES) * scale[None]
+        filt[g] = full.reshape(ctx, own, 2 * LANES) * scale[None, g * own : (g + 1) * own]
 
     for g in range(CHUNKS):
 
@@ -462,7 +520,7 @@
             return carry
 
         lax.fori_loop(0, ctx, decode, 0)
-        outer_forth()
+        outer_forth(values)
         full = product(spec[...].reshape(ctx * own, 2 * LANES), 0)
         real, imag = full[:, :LANES], full[:, LANES:]
         response = filt[g].reshape(ctx * own, 2 * LANES)
@@ -548,7 +606,8 @@
     order = pos_mid.shape[0]
     total_len = ctx * rows
     feat_rows = -(-(pos_in.shape[0] + 1) // 8) * 8
-    feats = jnp.asarray(position_table(total_len, feat_rows))
+    depth = -(-feat_rows * len(LEFT_PARTS) // 256) * 256
+    feats = jnp.asarray(stacked_positions(total_len, feat_rows, depth))
     inner = jnp.asarray(inner_tables())
     twist = jnp.asarray(twist_table(ctx, total_len))
     vmem = pl.BlockSpec(memory_space=pltpu.VMEM)
@@ -558,7 +617,7 @@
     wires = [pltpu.VMEM((CHUNKS, ctx, own, rows), bf16)] * 4
 
     def call(*refs):
-        return kernel(ctx, *refs)
+        return kernel(ctx, feat_rows, *refs)
 
     operands = (
         projected,
@@ -584,12 +643,15 @@
             pltpu.VMEM((3, width // LANES, EDGE + rows, LANES), f32),
             pltpu.VMEM((width // LANES, rows, LANES), f32),
             pltpu.VMEM((3, EDGE, width), bf16),
-            pltpu.VMEM((feat_rows, order), f32),
-            pltpu.VMEM((order, order), f32),
-            pltpu.VMEM((order, total_len), f32),
-            pltpu.VMEM((LANES, order), f32),
+            pltpu.VMEM((depth, LANES), f32),
+            pltpu.VMEM((len(LEFT_PARTS) * order, LANES), f32),
+            pltpu.VMEM((3 * order, LANES), f32),
+            pltpu.VMEM((order, depth), bf16),
+            pltpu.VMEM((order, len(LEFT_PARTS) * order), bf16),
+            pltpu.VMEM((LANES, 3 * order), f32),
             pltpu.VMEM((LANES, LANES), f32),
             pltpu.VMEM((ctx, own, LANES), f32),
+            pltpu.VMEM((CHUNKS, ctx, own, LANES), f32),
             pltpu.VMEM((ctx, own, 2 * LANES), f32),
             pltpu.VMEM((CHUNKS, ctx, own, 2 * LANES), f32),
             *wires,
@@ -600,12 +662,13 @@
             dma((CHUNKS, ctx)),
             dma((CHUNKS,)),
             dma((CHUNKS, ctx)),
+            pltpu.SemaphoreType.REGULAR((3, 2)),
         ],
         compiler_params=pltpu.CompilerParams(
-            collective_id=0, has_side_effects=True, vmem_limit_bytes=60 * 1024 * 1024
+            collective_id=0, has_side_effects=True, vmem_limit_bytes=40 * 1024 * 1024
         ),
         name="hyena",
-    )(*operands)
+    )(*[pltpu.with_memory_space_constraint(operand, pltpu.HBM) for operand in operands])
 
 
 def solution(mesh):

time: 71.3 us -> 66.4 us (0.931)
  Pallas kernels: 69.3 us -> 65.5 us
  local copies, waits for them, and re-layouts: 1.88 us -> 0.8 us
    pallas_call x1, Pallas kernels: 69.3 us -> 65.5 us  [body(): pl.pallas_call(call, out_shape=jax.ShapeDtypeStruct((rows, width), bf16),...]
    unnamed x1, local copies, waits for them, and re-layouts: 1.88 us -> 0.8 us
where the time goes in v2:
time: 66.4 us; the launch traced here: 66.3 us
  Pallas kernels  65.5 us (99%)
  local copies, waits for them, and re-layouts  0.8 us (1%)
    pallas_call x1, Pallas kernels, body(): pl.pallas_call(call, out_shape=jax.ShapeDtypeStruct((rows, width), bf16),...  65.5 us

profile of v2, /device:TPU:1, one launch (start us, length us, event | category | flops | bytes accessed | tf_op | source)
XLA Modules:
  0.0 66.3 jit_solution(4100687215948498609)
XLA Ops:
  0.0 65.5 %hyena.1 = bf16[128,2048]{1,0:T(8,128)(2,1)S(1)} custom-call(bf16[3,128,2048]{2,1,0:T(8,128)(2,1)} %refs_0_.1, f32[3,7,2048]{2,1,0:T(8,128)} %bitcast.5, f32[33,64]{1,0:T(8,128)} %refs_2_.1, f32[1,64]{1,0:T(1,128)} %bitcast.8, f32[1,64]{1,0:T(1,128)} %bitcast.9, f32[64,64]{1,0:T(8,128)} %refs_5_.1, f32[64,2048]{1,0:T(8,128)} %refs_6_.1, f32[1,2048]{1,0:T(1,128)} %bitcast.6, ...), custom_call_target="tpu_custom_call" | custom-call | tf_op jit(solution)/shard_map/hyena/pallas_call | solution.py:636
  65.5 0.8 %copy.14 = bf16[128,2048]{1,0:T(8,128)(2,1)} copy(bf16[128,2048]{1,0:T(8,128)(2,1)S(1)} %hyena.1) | data formatting | bytes 1048576

commit v3 on v2

--- a/solution.py
+++ b/solution.py
@@ -254,14 +254,27 @@
 
     pl.semaphore_wait(barrier, len(near))
 
-    rim_copy = pltpu.make_async_remote_copy(
-        src_ref=proj_any.at[:, pl.ds(rows - EDGE, EDGE), :],
-        dst_ref=rim,
-        send_sem=rim_send,
-        recv_sem=rim_recv,
-        device_id={"ctx": lax.rem(me + 1, ctx)},
-        device_id_type=MESH,
-    )
+    def rim_copy(stream):
+        return pltpu.make_async_remote_copy(
+            src_ref=proj_any.at[stream, pl.ds(rows - EDGE, EDGE), :],
+            dst_ref=rim.at[stream],
+            send_sem=rim_send.at[stream],
+            recv_sem=rim_recv.at[stream],
+            device_id={"ctx": lax.rem(me + 1, ctx)},
+            device_id_type=MESH,
+        )
+
+    def rim_start(*streams):
+        @pl.when(me < ctx - 1)
+        def _():
+            for stream in streams:
+                rim_copy(stream).start()
+
+    def rim_wait(*streams):
+        @pl.when(me > 0)
+        def _():
+            for stream in streams:
+                rim_copy(stream).wait_recv()
 
     def spread(step):
         away = 2**step
@@ -274,9 +287,7 @@
 
     spread(0)
 
-    @pl.when(me < ctx - 1)
-    def _():
-        rim_copy.start()
+    rim_start(0, 2)
 
     for fetch in fetches[: len(early)]:
         fetch.wait()
@@ -302,9 +313,7 @@
     def _():
         rim[...] = jnp.zeros_like(rim)
 
-    @pl.when(me > 0)
-    def _():
-        rim_copy.wait_recv()
+    rim_wait(0, 2)
 
     def forth(g, to):
         return pltpu.make_async_remote_copy(
@@ -350,7 +359,7 @@
                 make(g, to).start()
 
     def encode(n):
-        for stream in range(3):
+        for stream in (0, 2):
             wide[stream, n, 0:EDGE, :] = rim[stream, :, slab(n)].astype(jnp.float32)
         driven[n, 0:EDGE, :] = taps_sum(0, n, 0, EDGE) * taps_sum(2, n, 0, EDGE)
         code = coded(driven[n], OUT_REACH / bound(n), OUT_LOW, OUT_POWER)
@@ -386,6 +395,7 @@
 
     for g in range(1, CHUNKS):
         rest(g, forth)
+    rim_start(1)
     for g in range(CHUNKS):
         got_f[g, me] = send_f[g, me]
 
@@ -543,14 +553,17 @@
         lax.fori_loop(0, chips, pack, 0)
         got_r[g, me] = send_r[g, me]
 
+    rim_wait(1)
+
     def gate(n, carry):
+        wide[1, n, 0:EDGE, :] = rim[1, :, slab(n)].astype(jnp.float32)
         wide[1, n, EDGE : EDGE + rows, :] = taps_sum(1, n, 0, rows)
         return carry
 
     lax.fori_loop(0, chips, gate, 0)
 
     def finish(i, carry):
-        n = to_chip(chips - 1 - i)
+        n = to_chip(i)
         parts = []
         for c in range(2):
             frm = 2 * n + c
@@ -582,7 +595,8 @@
 
     @pl.when(me < ctx - 1)
     def _():
-        rim_copy.wait_send()
+        for stream in range(3):
+            rim_copy(stream).wait_send()
 
     for g in range(CHUNKS):
         for buffer, sem in ((send_f, f_send), (send_r, r_send)):
@@ -656,8 +670,8 @@
             pltpu.VMEM((CHUNKS, ctx, own, 2 * LANES), f32),
             *wires,
             dma((len(operands),)),
-            dma,
-            dma,
+            dma((3,)),
+            dma((3,)),
             dma((CHUNKS,)),
             dma((CHUNKS, ctx)),
             dma((CHUNKS,)),

time: 66.4 us -> 65.3 us (0.983)
  Pallas kernels: 65.5 us -> 64.4 us
    pallas_call x1, Pallas kernels: 65.5 us -> 64.4 us  [body(): pl.pallas_call(call, out_shape=jax.ShapeDtypeStruct((rows, width), bf16),...]
where the time goes in v3:
time: 65.3 us; the launch traced here: 65.2 us
  Pallas kernels  64.4 us (99%)
  local copies, waits for them, and re-layouts  0.8 us (1%)
    pallas_call x1, Pallas kernels, body(): pl.pallas_call(call, out_shape=jax.ShapeDtypeStruct((rows, width), bf16),...  64.4 us

profile of v3, /device:TPU:1, one launch (start us, length us, event | category | flops | bytes accessed | tf_op | source)
XLA Modules:
  0.0 65.2 jit_solution(7547486982383241330)
XLA Ops:
  0.0 64.4 %hyena.1 = bf16[128,2048]{1,0:T(8,128)(2,1)S(1)} custom-call(bf16[3,128,2048]{2,1,0:T(8,128)(2,1)} %refs_0_.1, f32[3,7,2048]{2,1,0:T(8,128)} %bitcast.5, f32[33,64]{1,0:T(8,128)} %refs_2_.1, f32[1,64]{1,0:T(1,128)} %bitcast.8, f32[1,64]{1,0:T(1,128)} %bitcast.9, f32[64,64]{1,0:T(8,128)} %refs_5_.1, f32[64,2048]{1,0:T(8,128)} %refs_6_.1, f32[1,2048]{1,0:T(1,128)} %bitcast.6, ...), custom_call_target="tpu_custom_call" | custom-call | tf_op jit(solution)/shard_map/hyena/pallas_call | solution.py:650
  64.4 0.8 %copy.14 = bf16[128,2048]{1,0:T(8,128)(2,1)} copy(bf16[128,2048]{1,0:T(8,128)(2,1)S(1)} %hyena.1) | data formatting | bytes 1048576
